TPU v7x, 256 devices: a whole 4x4x8 slice. The times are simulated.
256 devices in a mesh: dp: 32 (over y, x, core), tsp: 8 (over z).
Axes of the slice: x: 4, y: 4, z: 8, core: 2. Of those that a mesh axis runs over, the one named last changes fastest.
Arguments:
- tokens: bfloat16 [65536, 8192], P('dp', 'tsp'), may hold values from -6 to 6
- cotangent: bfloat16 [65536, 1024], P('dp', 'tsp'), may hold values from -6 to 6
- frozen_key_weight: bfloat16 [8192, 1024], P('tsp'), may hold values from -0.1875 to 0.1875
- adapter_down_weight: bfloat16 [64, 64, 8192], P('dp', None, 'tsp'), may hold values from -0.0625 to 0.0625
- adapter_up_weight: bfloat16 [64, 64, 1024], P('dp', None, 'tsp'), may hold values from -0.1875 to 0.1875
- adapter_place_table: int32 [64], replicated, may hold values from 0 to 63, as said below
- segment_adapter: int32 [512], P('dp'), may hold values from 0 to 63, as said below
- segment_live_count: int32 [512], P('dp'), may hold values from 1 to 128, as said below
Outputs:
- token_gradient: bfloat16 [65536, 8192], P('dp', 'tsp')
- down_grad: float32 [64, 64, 8192], P('dp', None, 'tsp')
- up_grad: float32 [64, 64, 1024], P('dp', None, 'tsp')
Inputs may be any that keep to these rules, and one draw needn't show every extreme that they name: A permutation: adapter a is held at place adapter_place_table[a], that is by the dp index adapter_place_table[a] // 2 as its entry adapter_place_table[a] % 2; the adapters' arrays and gradients are indexed by place. `segment_adapter`: the 16 segments of one dp index name at most one adapter held by any one dp index; an adapter may be named by several of them. `segment_live_count`: the live rows stand at the start of each segment; on every dp index some segment is full.
All inputs are finite; a program needn't handle non-finite values.
Results may differ from a plain program's by a relative error of at most 0.0034.
Values may be sent and summed in bfloat16 or wider, within the bound.
A program may use at most 128 MiB of HBM per device.

v0:
```python
import jax
import jax.numpy as jnp
from jax import lax
from jax.sharding import PartitionSpec as P

ADAPTER_SCALE = 2.0


def lookup(idents, mapping):
    matches = idents[:, None] == jnp.arange(mapping.shape[0], dtype=jnp.int32)[None, :]
    return jnp.sum(jnp.where(matches, mapping[None, :], 0), axis=1)


def on_device(
    tokens,
    cotangent,
    frozen_key_weight,
    adapter_down_weight,
    adapter_up_weight,
    adapter_place_table,
    segment_adapter,
    segment_live_count,
):
    dp_count = lax.axis_size("dp")
    places_per_device = adapter_down_weight.shape[0]
    rank_of_adapter = adapter_down_weight.shape[1]
    width_per_device = tokens.shape[1]
    key_dev = cotangent.shape[1]
    segments_per_device = segment_adapter.shape[0]
    segment_token_rows = tokens.shape[0] // segments_per_device
    adapter_places = lookup(segment_adapter, adapter_place_table)
    seg_owner = adapter_places // places_per_device
    seg_entry = adapter_places % places_per_device
    owner_hit = seg_owner[:, None] == jnp.arange(dp_count, dtype=jnp.int32)[None, :]
    wanted = jnp.max(jnp.where(owner_hit, seg_entry[:, None], -1), axis=0)
    incoming = lax.all_to_all(wanted[:, None], "dp", split_axis=0, concat_axis=0, tiled=True)[:, 0]
    serving_mesh = (
        incoming[:, None] == jnp.arange(places_per_device, dtype=jnp.int32)[None, :]
    ).astype(jnp.bfloat16)
    reply_down = jnp.einsum(
        "ap,phc->ahc", serving_mesh, adapter_down_weight, preferred_element_type=jnp.float32
    ).astype(jnp.bfloat16)
    reply_up = jnp.einsum(
        "hv,vun->hun", serving_mesh, adapter_up_weight, preferred_element_type=jnp.float32
    ).astype(jnp.bfloat16)
    fetched_down, fetched_up = (
        lax.all_to_all(reply_down, "dp", split_axis=0, concat_axis=0, tiled=True),
        lax.all_to_all(reply_up, "dp", split_axis=0, concat_axis=0, tiled=True),
    )
    picker = owner_hit.astype(jnp.bfloat16)
    segment_down_weight = jnp.einsum(
        "go,ord->grd", picker, fetched_down, preferred_element_type=jnp.float32
    ).astype(jnp.bfloat16)
    segment_up_weight = jnp.einsum(
        "go,ork->grk", picker, fetched_up, preferred_element_type=jnp.float32
    ).astype(jnp.bfloat16)
    seg_tokens = tokens.reshape(segments_per_device, segment_token_rows, width_per_device)
    seg_cotangent = cotangent.reshape(segments_per_device, segment_token_rows, key_dev)
    live_rows = (
        jnp.arange(segment_token_rows, dtype=jnp.int32)[None, :] < segment_live_count[:, None]
    ).astype(jnp.float32)
    partial_terms = jnp.concatenate(
        [
            jnp.einsum(
                "gtd,grd->gtr", seg_tokens, segment_down_weight, preferred_element_type=jnp.float32
            ),
            jnp.einsum(
                "gtk,grk->gtr", seg_cotangent, segment_up_weight, preferred_element_type=jnp.float32
            ),
        ],
        axis=2,
    )
    summed = lax.psum(partial_terms, "tsp")
    reduced_rows = (summed[:, :, :rank_of_adapter] * live_rows[:, :, None]).astype(jnp.bfloat16)
    gathered_weights = (summed[:, :, rank_of_adapter:] * live_rows[:, :, None]).astype(jnp.bfloat16)
    frozen_output = lax.dot_general(
        lax.all_gather(cotangent, "tsp", axis=1, tiled=True),
        frozen_key_weight,
        (((1,), (1,)), ((), ())),
        preferred_element_type=jnp.float32,
    )
    adapter_output = jnp.einsum(
        "wks,wsx->wkx", gathered_weights, segment_down_weight, preferred_element_type=jnp.float32
    )
    token_gradient = (
        frozen_output.reshape(segments_per_device, segment_token_rows, width_per_device)
        + ADAPTER_SCALE * adapter_output
    ) * live_rows[:, :, None]
    token_gradient = token_gradient.reshape(
        segments_per_device * segment_token_rows, width_per_device
    ).astype(jnp.bfloat16)
    gradient_scale = ADAPTER_SCALE / segment_token_rows
    segment_down_gradient = jnp.einsum(
        "upf,upb->ufb", gathered_weights, seg_tokens, preferred_element_type=jnp.float32
    )
    segment_up_gradient = jnp.einsum(
        "ija,ijn->ian", reduced_rows, seg_cotangent, preferred_element_type=jnp.float32
    )
    picker_f = owner_hit.astype(jnp.float32)
    slot_dgrad = (
        jnp.einsum("go,grd->ord", picker_f, segment_down_gradient, precision=lax.Precision.HIGHEST)
        * gradient_scale
    )
    slot_ugrad = (
        jnp.einsum("go,grk->ork", picker_f, segment_up_gradient, precision=lax.Precision.HIGHEST)
        * gradient_scale
    )
    slot_match = (wanted[:, None] == jnp.arange(places_per_device, dtype=jnp.int32)[None, :])[
        :, :, None, None
    ]
    dense_down = jnp.where(slot_match, slot_dgrad[:, None], 0.0).reshape(
        dp_count * places_per_device, rank_of_adapter, width_per_device
    )
    dense_up = jnp.where(slot_match, slot_ugrad[:, None], 0.0).reshape(
        dp_count * places_per_device, rank_of_adapter, key_dev
    )
    down_grad, up_grad = (
        lax.psum_scatter(dense_down, "dp", scatter_dimension=0, tiled=True),
        lax.psum_scatter(dense_up, "dp", scatter_dimension=0, tiled=True),
    )
    return (token_gradient, down_grad, up_grad)


def solution(mesh):
    placed = (
        P("dp", "tsp"),
        P("dp", "tsp"),
        P("tsp", None),
        P("dp", None, "tsp"),
        P("dp", None, "tsp"),
        P(),
        P("dp"),
        P("dp"),
    )
    return jax.shard_map(
        on_device,
        mesh=mesh,
        in_specs=placed,
        out_specs=(P("dp", "tsp"), P("dp", None, "tsp"), P("dp", None, "tsp")),
        check_vma=False,
    )
```

profile of v0, /device:TPU:2, one launch (start us, length us, event | category | flops | bytes accessed | tf_op | source)
XLA Modules:
  0.0 471.3 jit_solution(15498572598505192805)
XLA Ops:
  8.4 13.6 %all_to_all.19 = s32[32,1,1]{2,1,0:T(1,128)S(1)} all-to-all(s32[32,1,1]{2,1,0:T(1,128)S(1)} %copy.57), channel_id=1, replica_groups=mesh['dp'=32,'tsp'=8] {'dp'}, dimensions={0} | all-to-all | bytes 256 | tf_op jit(solution)/shard_map/all_to_all | solution.py:36
  22.6 1.1 convolution_convert_fusion.1
  24.8 5.0 %all-to-all-start.2 = ((bf16[32,64,128]{2,1,0:T(8,128)(2,1)}), bf16[32,64,128]{2,1,0:T(8,128)(2,1)S(1)}, u32[]{:S(2)}, u32[]{:S(2)}) async-start(bf16[32,64,128]{2,1,0:T(8,128)(2,1)} %copy.63), calls=%async_computation.2 | async-start | bytes 1048576 | tf_op jit(solution)/shard_map/all_to_all | solution.py:48
  29.8 2.3 convolution_convert_fusion
  32.0 4.3 copy.59
  36.4 3.9 all-to-all-done.2
  40.2 5.9 %all-to-all-start.1 = ((bf16[32,64,1024]{2,1,0:T(8,128)(2,1)}), bf16[32,64,1024]{2,1,0:T(8,128)(2,1)}, u32[]{:S(2)}, u32[]{:S(2)}) async-start(bf16[32,64,1024]{2,1,0:T(8,128)(2,1)} %copy.59), calls=%async_computation.1 | async-start | bytes 8388608 | tf_op jit(solution)/shard_map/all_to_all | solution.py:47
  47.3 50.4 %all-to-all-done.1 = bf16[32,64,1024]{2,1,0:T(8,128)(2,1)} async-done(((bf16[32,64,1024]{2,1,0:T(8,128)(2,1)}), bf16[32,64,1024]{2,1,0:T(8,128)(2,1)}, u32[]{:S(2)}, u32[]{:S(2)}) %all-to-all-start.1) | async-done | bytes 4194336 | tf_op jit(solution)/shard_map/all_to_all | solution.py:47
  97.7 6.9 %fusion.6 = bf16[16,64,1024]{2,0,1:T(8,128)(2,1)S(1)} fusion(bf16[32,64,1024]{2,1,0:T(8,128)(2,1)} %all-to-all-done.1, s32[16]{0:T(128)S(1)} %get-tuple-element.3), kind=kOutput, calls=%fused_computation.9 | convolution fusion | flops 68157952 | bytes 6291520 | tf_op jit(solution)/shard_map/go,ord->grd/dot_general | solution.py:51
  104.6 1.3 copy-done.1
  105.9 1.7 fusion.12
  107.6 1.1 pad_maximum_fusion
  109.8 75.4 %all-reduce.2.cloned.1.call-done = f32[16,128,128]{1,2,0:T(8,128)} async-done(((f32[16,128,128]{1,2,0:T(8,128)}), f32[16,128,128]{1,2,0:T(8,128)}) %all-reduce.2.cloned.1.call-update) | async-done | bytes 1048592 | tf_op jit(solution)/shard_map/psum | solution.py:73
  185.3 1.3 fusion.19
  188.1 1.5 bitcast_select_fusion.1
  189.9 2.9 fusion.24
  192.8 6.1 %broadcast_multiply_fusion = f32[32,64,1024]{2,0,1:T(8,128)S(1)} fusion(f32[16,64,1024]{2,1,0:T(8,128)S(1)} %fusion.24, s32[16]{0:T(128)S(1)} %get-tuple-element.3), kind=kOutput, calls=%fused_computation.6 | convolution fusion | flops 404750848 | bytes 12582976 | tf_op jit(solution)/shard_map/go,grd->ord/dot_general | solution.py:101
  198.9 8.1 %copy.68 = f32[32,64,1024]{2,1,0:T(8,128)} copy(f32[32,64,1024]{2,0,1:T(8,128)S(1)} %broadcast_multiply_fusion) | data formatting | bytes 16777216 | tf_op jit(solution)/shard_map/mul | solution.py:101
  207.0 12.7 %bitcast_select_fusion = f32[64,64,1024]{2,1,0:T(8,128)} fusion(f32[32,64,1024]{2,1,0:T(8,128)} %copy.68, pred[64]{0:T(512)(128)(4,1)S(1)} %eq.76), kind=kLoop, calls=%fused_computation | loop fusion | flops 4194304 | bytes 25165888 | tf_op jit(solution)/shard_map/jit(_where)/select_n | solution.py:111
  219.8 28.1 %all-gather.2.cloned.1.call-done = bf16[2048,1024]{1,0:T(8,128)(2,1)} async-done(((bf16[2048,128]{1,0:T(8,128)(2,1)}), bf16[2048,1024]{1,0:T(8,128)(2,1)}) %all-gather.2.cloned.1.call-update) | async-done | bytes 4194320 | tf_op jit(solution)/shard_map/all_gather | solution.py:77
  247.9 6.5 %fusion.42 = f32[2048,1024]{1,0:T(8,128)S(1)} fusion(bf16[2048,1024]{1,0:T(8,128)(2,1)} %all-gather.2.cloned.1.call-done, bf16[1024,1024]{1,0:T(8,128)(2,1)S(1)} %copy-done), kind=kOutput, calls=%fused_computation.53 | convolution fusion | flops 4294967296 | bytes 14680064 | tf_op jit(solution)/shard_map/dot_general | solution.py:76
  254.4 5.2 %multiply_convert_fusion = bf16[16,128,1024]{2,1,0:T(8,128)(2,1)} fusion(f32[16,128,1024]{2,1,0:T(8,128)S(1)} %bitcast.32, f32[16,128]{1,0:T(8,128)S(1)} %fusion.33, bf16[16,64,1024]{2,0,1:T(8,128)(2,1)S(1)} %copy-done.2, f32[16,128,128]{1,2,0:T(8,128)S(1)} %copy-done.6), kind=kOutput, calls=%fused_computation.1 | convolution fusion | flops 277086208 | bytes 15220736 | tf_op jit(solution)/shard_map/wks,wsx->wkx/dot_general | solution.py:82
  259.7 77.8 %reduce-scatter.5.cloned.1.call-done = f32[2,64,128]{2,1,0:T(8,128)} async-done(((f32[64,64,128]{2,1,0:T(8,128)}), f32[2,64,128]{2,1,0:T(8,128)}) %reduce-scatter.5.cloned.1.call-update) | async-done | bytes 65552 | tf_op jit(solution)/shard_map/reduce_scatter | solution.py:119
  337.5 127.2 %reduce-scatter.3.cloned.1.call-done = f32[2,64,1024]{2,1,0:T(8,128)} async-done(((f32[64,64,1024]{2,1,0:T(8,128)}), f32[2,64,1024]{2,1,0:T(8,128)}) %reduce-scatter.3.cloned.1.call-update) | async-done | bytes 524304 | tf_op jit(solution)/shard_map/reduce_scatter | solution.py:118
  (36 shorter events, 6.8 us)
Async XLA Ops:
  7.2 240.8 %copy-start = (bf16[1024,1024]{1,0:T(8,128)(2,1)S(1)}, bf16[1024,1024]{1,0:T(8,128)(2,1)}, u32[]{:S(2)}) copy-start(bf16[1024,1024]{1,0:T(8,128)(2,1)} %param.10) | copy-start | bytes 6291460
  24.8 15.5 %all-to-all-start.2 = ((bf16[32,64,128]{2,1,0:T(8,128)(2,1)}), bf16[32,64,128]{2,1,0:T(8,128)(2,1)S(1)}, u32[]{:S(2)}, u32[]{:S(2)}) async-start(bf16[32,64,128]{2,1,0:T(8,128)(2,1)} %copy.63), calls=%async_computation.2 | async-start | bytes 1048576 | tf_op jit(solution)/shard_map/all_to_all | solution.py:48
  36.4 10.4 %copy-start.4 = (bf16[2048,128]{1,0:T(8,128)(2,1)S(1)}, bf16[2048,128]{1,0:T(8,128)(2,1)}, u32[]{:S(2)}) copy-start(bf16[2048,128]{1,0:T(8,128)(2,1)} %param.9) | copy-start | bytes 1572868
  40.2 57.4 %all-to-all-start.1 = ((bf16[32,64,1024]{2,1,0:T(8,128)(2,1)}), bf16[32,64,1024]{2,1,0:T(8,128)(2,1)}, u32[]{:S(2)}, u32[]{:S(2)}) async-start(bf16[32,64,1024]{2,1,0:T(8,128)(2,1)} %copy.59), calls=%async_computation.1 | async-start | bytes 8388608 | tf_op jit(solution)/shard_map/all_to_all | solution.py:47
  46.2 139.1 %all-reduce.2.cloned.1.call-start = ((), (), s32[]{:S(2)}) async-start(), calls=%async_computation.6 | async-start | bytes 2097152 | tf_op jit(solution)/shard_map/psum | solution.py:73
  97.7 8.2 %copy-start.3 = (bf16[2048,1024]{1,0:T(8,128)(2,1)S(1)}, bf16[2048,1024]{1,0:T(8,128)(2,1)}, u32[]{:S(2)}) copy-start(bf16[2048,1024]{1,0:T(8,128)(2,1)} %param.8) | copy-start | bytes 12582916
  104.6 1.3 copy-start.1
  105.9 3.9 copy-start.7
  105.9 79.4 %copy-start.5 = (bf16[2048,128]{1,0:T(8,128)(2,1)S(1)}, bf16[2048,128]{1,0:T(8,128)(2,1)}, u32[]{:S(2)}) copy-start(bf16[2048,128]{1,0:T(8,128)(2,1)} %param.9) | copy-start | bytes 1572868
  108.8 139.1 %all-gather.2.cloned.1.call-start = ((), (), s32[]{:S(2)}) async-start(), calls=%async_computation.5 | async-start | bytes 4718592 | tf_op jit(solution)/shard_map/all_gather | solution.py:77
  109.5 228.0 %reduce-scatter.5.cloned.1.call-start = ((), (), s32[]{:S(2)}) async-start(), calls=%async_computation.8 | async-start | bytes 2162688 | tf_op jit(solution)/shard_map/reduce_scatter | solution.py:119
  186.6 3.4 copy-start.6
  189.7 275.1 %reduce-scatter.3.cloned.1.call-start = ((), (), s32[]{:S(2)}) async-start(), calls=%async_computation.7 | async-start | bytes 17301504 | tf_op jit(solution)/shard_map/reduce_scatter | solution.py:118
  247.9 6.5 %copy-start.2 = (bf16[16,64,1024]{2,0,1:T(8,128)(2,1)S(1)}, bf16[16,64,1024]{2,0,1:T(8,128)(2,1)}, u32[]{:S(2)}) copy-start(bf16[16,64,1024]{2,0,1:T(8,128)(2,1)} %copy-done.1) | copy-start | bytes 6291460
Sparse Core Ops, SparseCore 0:
  108.9 76.3 all-reduce.1
  187.0 60.8 all-gather.1
  252.3 85.1 reduce-scatter.4
  342.1 122.5 reduce-scatter.2
where the time goes:
time: 472 us; the launch traced here: 471 us
  waiting for transfers between devices  364 us (77%)
  matrix products  35.8 us (8%)
  other arithmetic  17.3 us (4%)
  local copies, waits for them, and re-layouts  15.6 us (3%)
  between operations  13.9 us (3%)
  blocking collectives  13.6 us (3%)
  starting transfers between devices  11.5 us (2%)
    reduce_scatter x1, waiting for transfers between devices, on_device(): lax.psum_scatter(dense_down, 'dp', scatter_dimension=0, tiled=True)  127 us
    reduce_scatter x1, waiting for transfers between devices, on_device(): lax.psum_scatter(dense_up, 'dp', scatter_dimension=0, tiled=True)  77.8 us
    psum x1, waiting for transfers between devices, on_device(): summed = lax.psum(partial_terms, 'tsp')  75.4 us
    all_to_all x1, waiting for transfers between devices, on_device(): lax.all_to_all(reply_down, 'dp', split_axis=0, concat_axis=0, tiled=True)  50.4 us
    all_gather x1, waiting for transfers between devices, on_device(): lax.all_gather(cotangent, 'tsp', axis=1, tiled=True)  28.1 us
    all_to_all x1, blocking collectives, on_device(): lax.all_to_all(wanted[:, None], 'dp', split_axis=0, concat_axis=0, tiled=...  13.6 us
    select_n x1, other arithmetic, on_device(): jnp.where(slot_match, slot_dgrad[:, None], 0.0)  12.7 us
  transfers between devices with their start and end apart: 6, of which 6 were waited for; matrix products, arithmetic and copies ran while one was open for 11% of the time, Pallas kernels for 0%

commit v1 on v0

--- a/solution.py
+++ b/solution.py
@@ -4,6 +4,12 @@
 from jax.sharding import PartitionSpec as P
 
 ADAPTER_SCALE = 2.0
+
+
+def add_all(x, mesh_axis):
+    parts = lax.all_gather(x, mesh_axis, axis=0, tiled=False)
+    total = parts.sum(axis=0)
+    return total
 
 
 def lookup(idents, mapping):
@@ -70,7 +76,7 @@
         ],
         axis=2,
     )
-    summed = lax.psum(partial_terms, "tsp")
+    summed = add_all(partial_terms, "tsp")
     reduced_rows = (summed[:, :, :rank_of_adapter] * live_rows[:, :, None]).astype(jnp.bfloat16)
     gathered_weights = (summed[:, :, rank_of_adapter:] * live_rows[:, :, None]).astype(jnp.bfloat16)
     frozen_output = lax.dot_general(

time: 472 us -> 490 us (1.038)
  waiting for transfers between devices: 364 us -> 372 us
  local copies, waits for them, and re-layouts: 15.6 us -> 22 us
    all_gather x0 -> x1, waiting for transfers between devices: none -> 93.5 us  [add_all(): parts = lax.all_gather(x, mesh_axis, axis=0, tiled=False)]
    psum x1 -> x0, waiting for transfers between devices: 75.4 us -> none  [on_device(): summed = lax.psum(partial_terms, 'tsp')]
    all_gather x1, waiting for transfers between devices: 28.1 us -> 19.4 us  [on_device(): lax.all_gather(cotangent, 'tsp', axis=1, tiled=True)]
  transfers between devices with their start and end apart: 6 -> 6, of which waited for: 6 -> 6; matrix products, arithmetic and copies ran while one was open for 11% -> 13% of each run, Pallas kernels for 0% -> 0%
where the time goes in v1:
time: 490 us
  waiting for transfers between devices  372 us (76%)
  matrix products  36.6 us (7%)
  local copies, waits for them, and re-layouts  22 us (4%)
  other arithmetic  20.1 us (4%)
  between operations  13.9 us (3%)
  blocking collectives  13.6 us (3%)
  starting transfers between devices  11.5 us (2%)
    reduce_scatter x1, waiting for transfers between devices, on_device(): lax.psum_scatter(dense_down, 'dp', scatter_dimension=0, tiled=True)  127 us
    all_gather x1, waiting for transfers between devices, add_all(): parts = lax.all_gather(x, mesh_axis, axis=0, tiled=False)  93.5 us
    reduce_scatter x1, waiting for transfers between devices, on_device(): lax.psum_scatter(dense_up, 'dp', scatter_dimension=0, tiled=True)  77.6 us
    all_to_all x1, waiting for transfers between devices, on_device(): lax.all_to_all(reply_down, 'dp', split_axis=0, concat_axis=0, tiled=True)  49.6 us
    all_gather x1, waiting for transfers between devices, on_device(): lax.all_gather(cotangent, 'tsp', axis=1, tiled=True)  19.4 us
    all_to_all x1, blocking collectives, on_device(): lax.all_to_all(wanted[:, None], 'dp', split_axis=0, concat_axis=0, tiled=...  13.6 us
    select_n x1, other arithmetic, on_device(): jnp.where(slot_match, slot_dgrad[:, None], 0.0)  12.4 us
  transfers between devices with their start and end apart: 6, of which 6 were waited for; matrix products, arithmetic and copies ran while one was open for 13% of the time, Pallas kernels for 0%

profile of v1, /device:TPU:2, one launch (start us, length us, event | category | flops | bytes accessed | tf_op | source)
XLA Modules:
  0.0 489.7 jit_solution(4967920647770230533)
XLA Ops:
  8.4 13.6 %all_to_all.19 = s32[32,1,1]{2,1,0:T(1,128)S(1)} all-to-all(s32[32,1,1]{2,1,0:T(1,128)S(1)} %copy.81), channel_id=1, replica_groups=mesh['dp'=32,'tsp'=8] {'dp'}, dimensions={0} | all-to-all | bytes 256 | tf_op jit(solution)/shard_map/all_to_all | solution.py:42
  24.8 5.0 %all-to-all-start.2 = ((bf16[32,64,128]{2,1,0:T(8,128)(2,1)}), bf16[32,64,128]{2,1,0:T(8,128)(2,1)S(1)}, u32[]{:S(2)}, u32[]{:S(2)}) async-start(bf16[32,64,128]{2,1,0:T(8,128)(2,1)} %copy.87), calls=%async_computation.2 | async-start | bytes 1048576 | tf_op jit(solution)/shard_map/all_to_all | solution.py:54
  29.8 2.3 convolution_convert_fusion
  32.0 4.3 copy.83
  36.4 3.9 all-to-all-done.2
  40.2 5.9 %all-to-all-start.1 = ((bf16[32,64,1024]{2,1,0:T(8,128)(2,1)}), bf16[32,64,1024]{2,1,0:T(8,128)(2,1)}, u32[]{:S(2)}, u32[]{:S(2)}) async-start(bf16[32,64,1024]{2,1,0:T(8,128)(2,1)} %copy.83), calls=%async_computation.1 | async-start | bytes 8388608 | tf_op jit(solution)/shard_map/all_to_all | solution.py:53
  48.1 49.6 %all-to-all-done.1 = bf16[32,64,1024]{2,1,0:T(8,128)(2,1)} async-done(((bf16[32,64,1024]{2,1,0:T(8,128)(2,1)}), bf16[32,64,1024]{2,1,0:T(8,128)(2,1)}, u32[]{:S(2)}, u32[]{:S(2)}) %all-to-all-start.1) | async-done | bytes 4194336 | tf_op jit(solution)/shard_map/all_to_all | solution.py:53
  97.7 6.9 %fusion.6 = bf16[16,64,1024]{2,0,1:T(8,128)(2,1)S(1)} fusion(bf16[32,64,1024]{2,1,0:T(8,128)(2,1)} %all-to-all-done.1, s32[16]{0:T(128)S(1)} %get-tuple-element.5), kind=kOutput, calls=%fused_computation.9 | convolution fusion | flops 68157952 | bytes 6291520 | tf_op jit(solution)/shard_map/go,ord->grd/dot_general | solution.py:57
  105.9 1.7 fusion.12
  110.2 93.5 %all-gather.6.cloned.1.call-done = f32[128,128,128]{2,1,0:T(8,128)} async-done(((f32[16,128,128]{2,1,0:T(8,128)}), f32[128,128,128]{2,1,0:T(8,128)}) %all-gather.6.cloned.1.call-update) | async-done | bytes 8388624 | tf_op jit(solution)/shard_map/all_gather | solution.py:10
  203.8 4.2 reduce_sum.19
  207.9 1.7 fusion.37
  209.6 1.5 copy.99
  214.0 1.5 bitcast_select_fusion.1
  215.8 1.6 copy.98
  217.4 2.9 fusion.21
  220.3 6.1 %broadcast_multiply_fusion = f32[32,64,1024]{2,0,1:T(8,128)S(1)} fusion(f32[16,64,1024]{2,1,0:T(8,128)S(1)} %fusion.21, s32[16]{0:T(128)S(1)} %get-tuple-element.5), kind=kOutput, calls=%fused_computation.6 | convolution fusion | flops 404750848 | bytes 12582976 | tf_op jit(solution)/shard_map/go,grd->ord/dot_general | solution.py:107
  226.4 8.4 %copy.94 = f32[32,64,1024]{2,1,0:T(8,128)} copy(f32[32,64,1024]{2,0,1:T(8,128)S(1)} %broadcast_multiply_fusion) | data formatting | bytes 16777216 | tf_op jit(solution)/shard_map/mul | solution.py:107
  234.7 12.4 %bitcast_select_fusion = f32[64,64,1024]{2,1,0:T(8,128)} fusion(f32[32,64,1024]{2,1,0:T(8,128)} %copy.94, pred[64]{0:T(512)(128)(4,1)S(1)} %eq.76), kind=kLoop, calls=%fused_computation | loop fusion | flops 4194304 | bytes 25165888 | tf_op jit(solution)/shard_map/jit(_where)/select_n | solution.py:117
  247.2 19.4 %all-gather.4.cloned.1.call-done = bf16[2048,1024]{1,0:T(8,128)(2,1)} async-done(((bf16[2048,128]{1,0:T(8,128)(2,1)}), bf16[2048,1024]{1,0:T(8,128)(2,1)}) %all-gather.4.cloned.1.call-update) | async-done | bytes 4194320 | tf_op jit(solution)/shard_map/all_gather | solution.py:83
  266.6 6.5 %fusion.38 = f32[2048,1024]{1,0:T(8,128)S(1)} fusion(bf16[2048,1024]{1,0:T(8,128)(2,1)} %all-gather.4.cloned.1.call-done, bf16[1024,1024]{1,0:T(8,128)(2,1)S(1)} %copy-done), kind=kOutput, calls=%fused_computation.52 | convolution fusion | flops 4294967296 | bytes 14680064 | tf_op jit(solution)/shard_map/dot_general | solution.py:82
  273.1 5.2 %multiply_convert_fusion = bf16[16,128,1024]{2,1,0:T(8,128)(2,1)} fusion(f32[16,128,1024]{2,1,0:T(8,128)S(1)} %bitcast.33, f32[16,128]{1,0:T(8,128)S(1)} %fusion.28, bf16[16,64,1024]{2,0,1:T(8,128)(2,1)S(1)} %copy-done.2, f32[16,128,64]{1,2,0:T(8,128)S(1)} %copy.98), kind=kOutput, calls=%fused_computation.1 | convolution fusion | flops 277086208 | bytes 15212544 | tf_op jit(solution)/shard_map/wks,wsx->wkx/dot_general | solution.py:88
  278.3 77.6 %reduce-scatter.5.cloned.1.call-done = f32[2,64,128]{2,1,0:T(8,128)} async-done(((f32[64,64,128]{2,1,0:T(8,128)}), f32[2,64,128]{2,1,0:T(8,128)}) %reduce-scatter.5.cloned.1.call-update) | async-done | bytes 65552 | tf_op jit(solution)/shard_map/reduce_scatter | solution.py:125
  355.9 127.2 %reduce-scatter.3.cloned.1.call-done = f32[2,64,1024]{2,1,0:T(8,128)} async-done(((f32[64,64,1024]{2,1,0:T(8,128)}), f32[2,64,1024]{2,1,0:T(8,128)}) %reduce-scatter.3.cloned.1.call-update) | async-done | bytes 524304 | tf_op jit(solution)/shard_map/reduce_scatter | solution.py:124
  (39 shorter events, 12.9 us)
Async XLA Ops:
  7.2 259.4 %copy-start = (bf16[1024,1024]{1,0:T(8,128)(2,1)S(1)}, bf16[1024,1024]{1,0:T(8,128)(2,1)}, u32[]{:S(2)}) copy-start(bf16[1024,1024]{1,0:T(8,128)(2,1)} %param.10) | copy-start | bytes 6291460
  24.8 15.5 %all-to-all-start.2 = ((bf16[32,64,128]{2,1,0:T(8,128)(2,1)}), bf16[32,64,128]{2,1,0:T(8,128)(2,1)S(1)}, u32[]{:S(2)}, u32[]{:S(2)}) async-start(bf16[32,64,128]{2,1,0:T(8,128)(2,1)} %copy.87), calls=%async_computation.2 | async-start | bytes 1048576 | tf_op jit(solution)/shard_map/all_to_all | solution.py:54
  36.4 10.4 %copy-start.4 = (bf16[2048,128]{1,0:T(8,128)(2,1)S(1)}, bf16[2048,128]{1,0:T(8,128)(2,1)}, u32[]{:S(2)}) copy-start(bf16[2048,128]{1,0:T(8,128)(2,1)} %param.9) | copy-start | bytes 1572868
  40.2 57.4 %all-to-all-start.1 = ((bf16[32,64,1024]{2,1,0:T(8,128)(2,1)}), bf16[32,64,1024]{2,1,0:T(8,128)(2,1)}, u32[]{:S(2)}, u32[]{:S(2)}) async-start(bf16[32,64,1024]{2,1,0:T(8,128)(2,1)} %copy.83), calls=%async_computation.1 | async-start | bytes 8388608 | tf_op jit(solution)/shard_map/all_to_all | solution.py:53
  46.2 157.6 %all-gather.6.cloned.1.call-start = ((), (), s32[]{:S(2)}) async-start(), calls=%async_computation.8 | async-start | bytes 9437184 | tf_op jit(solution)/shard_map/all_gather | solution.py:10
  97.7 8.2 %copy-start.3 = (bf16[2048,1024]{1,0:T(8,128)(2,1)S(1)}, bf16[2048,1024]{1,0:T(8,128)(2,1)}, u32[]{:S(2)}) copy-start(bf16[2048,1024]{1,0:T(8,128)(2,1)} %param.8) | copy-start | bytes 12582916
  104.6 1.3 copy-start.1
  104.6 3.1 copy-start.5
  107.6 2.5 copy-start.6
  109.1 157.4 %all-gather.4.cloned.1.call-start = ((), (), s32[]{:S(2)}) async-start(), calls=%async_computation.5 | async-start | bytes 4718592 | tf_op jit(solution)/shard_map/all_gather | solution.py:83
  109.9 246.0 %reduce-scatter.5.cloned.1.call-start = ((), (), s32[]{:S(2)}) async-start(), calls=%async_computation.7 | async-start | bytes 2162688 | tf_op jit(solution)/shard_map/reduce_scatter | solution.py:125
  215.6 267.6 %reduce-scatter.3.cloned.1.call-start = ((), (), s32[]{:S(2)}) async-start(), calls=%async_computation.6 | async-start | bytes 17301504 | tf_op jit(solution)/shard_map/reduce_scatter | solution.py:124
  266.6 6.5 %copy-start.2 = (bf16[16,64,1024]{2,0,1:T(8,128)(2,1)S(1)}, bf16[16,64,1024]{2,0,1:T(8,128)(2,1)}, u32[]{:S(2)}) copy-start(bf16[16,64,1024]{2,0,1:T(8,128)(2,1)} %copy-done.1) | copy-start | bytes 6291460
Sparse Core Ops, SparseCore 0:
  109.3 94.4 all-gather.5
  205.5 61.0 all-gather.3
  271.0 84.9 reduce-scatter.4
  360.6 122.5 reduce-scatter.2
